TPU v7x, 32 devices: a whole 2x2x4 slice. The times are simulated.
32 devices in a mesh: dp: 4 (over y, x), expert: 8 (over z, core).
Axes of the slice: x: 2, y: 2, z: 4, core: 2. Of those that a mesh axis runs over, the one named last changes fastest.
Arguments:
- tokens: bfloat16 [4096, 2048], P(('dp', 'expert')), may hold values from -6 to 6
- out_grad: bfloat16 [4096, 2048], P(('dp', 'expert')), may hold values from -6 to 6
- routes: int32 [4096, 4], P(('dp', 'expert')), may hold values from 0 to 7, all different within a row; in each aligned block of 128 rows (0 to 127, 128 to 255, ...) at most 72 rows name the same one
- gate_values: float32 [4096, 4], P(('dp', 'expert')), may hold values from 0.05 to 1
- w_gate: bfloat16 [8, 2048, 768], P('expert', 'dp'), may hold values from -0.125 to 0.125
- w_up: bfloat16 [8, 2048, 768], P('expert', 'dp'), may hold values from -0.125 to 0.125
- w_down: bfloat16 [8, 768, 2048], P('expert', None, 'dp'), may hold values from -0.21875 to 0.21875
Outputs:
- input_grad: bfloat16 [4096, 2048], P(('dp', 'expert'))
- gate_grad: bfloat16 [8, 2048, 768], P('expert', 'dp')
- up_grad: bfloat16 [8, 2048, 768], P('expert', 'dp')
- down_grad: bfloat16 [8, 768, 2048], P('expert', None, 'dp')
Inputs may be any that keep to these rules, and one draw needn't show every extreme that they name: `routes`: each token names 4 different experts. Among the 128 tokens of one device (aligned blocks of 128 tokens) no expert is named by more than 72 tokens, and in every draw some device names some expert exactly 72 times.
All inputs are finite; a program needn't handle non-finite values.
Results may differ from a plain program's by a relative error of at most 0.0095.
Values may be sent and summed in bfloat16 or wider, within the bound.
No kernel may reach another device: no remote copies, remote signals or barrier semaphores. Data moves between devices by JAX's collectives and lax.ppermute only.
A program may use at most 128 MiB of HBM per device.

v0:
```python
import jax
import jax.numpy as jnp
from jax import lax
from jax.sharding import PartitionSpec as P


def local(tokens, out_grad, routes, gate_values, w_gate, w_up, w_down):
    tok_rows, model_width = tokens.shape
    top_count = routes.shape[1]
    group_count = lax.axis_size("expert")
    local_count = w_gate.shape[0]
    expert_count = group_count * local_count
    hidden_units = w_gate.shape[2]
    capacity = min(tok_rows, max(2, 9 * tok_rows * top_count // (8 * expert_count)))
    pair_count = tok_rows * top_count
    slot_count = group_count * capacity
    expert_of = routes.reshape(-1)
    onehot = (expert_of[:, None] == jnp.arange(expert_count, dtype=jnp.int32)[None, :]).astype(
        jnp.int32
    )
    before = jnp.cumsum(onehot, axis=0) - onehot
    placed = jnp.sum(before * onehot, axis=1)
    slot_of = expert_of * capacity + placed
    slot_table = jnp.full((expert_count * capacity,), pair_count, jnp.int32)
    slot_table = slot_table.at[slot_of].set(jnp.arange(pair_count, dtype=jnp.int32))
    filled = slot_table < pair_count
    source = jnp.where(filled, slot_table, 0)
    owner_row = source // top_count
    send_x = jnp.where(filled[:, None], tokens[owner_row], jnp.zeros((), jnp.bfloat16))
    scaled = gate_values.reshape(-1)[source][:, None] * out_grad[owner_row].astype(jnp.float32)
    send_dy = jnp.where(filled[:, None], scaled, 0.0).astype(jnp.bfloat16)
    send_x = send_x.reshape(expert_count, capacity, model_width)
    send_dy = send_dy.reshape(expert_count, capacity, model_width)
    recv_x, recv_dy = (
        lax.all_to_all(send_x, "expert", split_axis=0, concat_axis=0, tiled=True),
        lax.all_to_all(send_dy, "expert", split_axis=0, concat_axis=0, tiled=True),
    )

    def to_local(stacked):
        shaped = stacked.reshape(group_count, local_count, capacity, model_width)
        return shaped.transpose(1, 0, 2, 3).reshape(local_count, slot_count, model_width)

    slot_x = to_local(recv_x)
    slot_dy = to_local(recv_dy)
    part_x = slot_x
    gate_term = jnp.einsum(
        "asd,adf->asf",
        part_x,
        lax.all_gather(w_gate, "dp", axis=1, tiled=True),
        preferred_element_type=jnp.float32,
    )
    up_term = jnp.einsum(
        "asd,adf->asf",
        part_x,
        lax.all_gather(w_up, "dp", axis=1, tiled=True),
        preferred_element_type=jnp.float32,
    )
    full_gate, full_up, full_down = (
        lax.all_gather(w_gate, "dp", axis=1, tiled=True),
        lax.all_gather(w_up, "dp", axis=1, tiled=True),
        lax.all_gather(w_down, "dp", axis=2, tiled=True),
    )
    sigma = jax.nn.sigmoid(gate_term)
    active = gate_term * sigma
    activated = (active * up_term).astype(jnp.bfloat16)
    back_hidden = jnp.einsum("asd,afd->asf", slot_dy, full_down, preferred_element_type=jnp.float32)
    up_delta = (back_hidden * active).astype(jnp.bfloat16)
    gate_delta = (back_hidden * up_term * sigma * (1.0 + gate_term * (1.0 - sigma))).astype(
        jnp.bfloat16
    )
    pair_grad = (
        jnp.einsum("asf,adf->asd", gate_delta, full_gate, preferred_element_type=jnp.float32)
        + jnp.einsum("asf,adf->asd", up_delta, full_up, preferred_element_type=jnp.float32)
    ).astype(jnp.bfloat16)
    send_back = pair_grad.reshape(local_count, group_count, capacity, model_width).transpose(
        1, 0, 2, 3
    )
    send_back = send_back.reshape(expert_count, capacity, model_width)
    returned = lax.all_to_all(send_back, "expert", split_axis=0, concat_axis=0, tiled=True)
    per_pair = returned.reshape(expert_count * capacity, model_width)[slot_of].astype(jnp.float32)
    input_grad = jnp.sum(per_pair.reshape(tok_rows, top_count, model_width), axis=1).astype(
        jnp.bfloat16
    )
    block_width = local_count * hidden_units
    share_width = model_width // lax.axis_size("dp")
    part_x = slot_x
    term_gate = jnp.einsum("asd,asf->daf", part_x, gate_delta, preferred_element_type=jnp.float32)
    term_up = jnp.einsum("asd,asf->daf", part_x, up_delta, preferred_element_type=jnp.float32)
    term_down = jnp.einsum("asd,asf->daf", slot_dy, activated, preferred_element_type=jnp.float32)
    shares = lax.psum_scatter(
        jnp.concatenate(
            [
                term_gate.reshape(lax.axis_size("dp") * share_width, block_width),
                term_up.reshape(lax.axis_size("dp") * share_width, block_width),
                term_down.reshape(lax.axis_size("dp") * share_width, block_width),
            ],
            axis=1,
        ).astype(jnp.bfloat16),
        "dp",
        scatter_dimension=0,
        tiled=True,
    ).astype(jnp.float32)
    share_rows = shares.shape[0]

    def unpack(which):
        return shares[:, which * block_width : (which + 1) * block_width].reshape(
            share_rows, local_count, hidden_units
        )

    gate_grad = unpack(0).transpose(1, 0, 2).astype(jnp.bfloat16)
    up_grad = unpack(1).transpose(1, 0, 2).astype(jnp.bfloat16)
    down_grad = unpack(2).transpose(1, 2, 0).astype(jnp.bfloat16)
    return (input_grad, gate_grad, up_grad, down_grad)


def solution(mesh):
    return jax.shard_map(
        local,
        mesh=mesh,
        in_specs=(
            P(("dp", "expert"), None),
            P(("dp", "expert"), None),
            P(("dp", "expert"), None),
            P(("dp", "expert"), None),
            P("expert", "dp", None),
            P("expert", "dp", None),
            P("expert", None, "dp"),
        ),
        out_specs=(
            P(("dp", "expert"), None),
            P("expert", "dp", None),
            P("expert", "dp", None),
            P("expert", None, "dp"),
        ),
        check_vma=False,
    )
```

profile of v0, /device:TPU:0, one launch (start us, length us, event | category | flops | bytes accessed | tf_op | source)
XLA Modules:
  0.0 274.2 jit_solution(3252684024728993636)
XLA Ops:
  10.6 1.1 reduce-window.6
  12.1 2.4 scatter_custom_fusion
  14.7 3.4 %gather_fusion.2 = bf16[576,2048]{1,0:T(8,128)(2,1)S(1)} fusion(bf16[128,2048]{1,0:T(8,128)(2,1)S(1)} %copy-done, s32[1024]{0:T(1024)S(1)} %get-tuple-element.19), kind=kCustom, calls=%fused_computation.2 | custom fusion | bytes 4720896 | tf_op jit(solution)/shard_map/gather | solution.py:29
  18.1 1.6 broadcast_select_fusion
  19.7 6.5 %all-to-all-start.1 = ((bf16[8,72,2048]{2,1,0:T(8,128)(2,1)}), bf16[8,72,2048]{2,1,0:T(8,128)(2,1)}, u32[]{:S(2)}, u32[]{:S(2)}) async-start(bf16[8,72,2048]{2,1,0:T(8,128)(2,1)} %broadcast_select_fusion), calls=%async_computation.1 | async-start | bytes 4718592 | tf_op jit(solution)/shard_map/all_to_all | solution.py:35
  26.5 4.0 %gather_fusion = f32[576]{0:T(1024)S(1)} fusion(f32[512]{0:T(512)S(1)} %reshape.168, s32[1024]{0:T(1024)S(1)} %get-tuple-element.20), kind=kCustom, calls=%fused_computation | custom fusion | bytes 6912 | tf_op jit(solution)/shard_map/gather | solution.py:30
  30.5 3.4 %gather_fusion.1 = bf16[576,2048]{1,0:T(8,128)(2,1)S(1)} fusion(bf16[128,2048]{1,0:T(8,128)(2,1)S(1)} %copy-done.2, s32[1024]{0:T(1024)S(1)} %get-tuple-element.19), kind=kCustom, calls=%fused_computation.1 | custom fusion | bytes 4720896 | tf_op jit(solution)/shard_map/gather | solution.py:30
  33.9 2.0 fusion.1
  36.0 45.0 %all-to-all-done.1 = bf16[8,72,2048]{2,1,0:T(8,128)(2,1)} async-done(((bf16[8,72,2048]{2,1,0:T(8,128)(2,1)}), bf16[8,72,2048]{2,1,0:T(8,128)(2,1)}, u32[]{:S(2)}, u32[]{:S(2)}) %all-to-all-start.1) | async-done | bytes 2359328 | tf_op jit(solution)/shard_map/all_to_all | solution.py:35
  81.0 3.7 %all-to-all-start = ((bf16[8,72,2048]{2,1,0:T(8,128)(2,1)}), bf16[8,72,2048]{2,1,0:T(8,128)(2,1)S(1)}, u32[]{:S(2)}, u32[]{:S(2)}) async-start(bf16[8,72,2048]{2,1,0:T(8,128)(2,1)} %fusion.1), calls=%async_computation | async-start | bytes 4718592 | tf_op jit(solution)/shard_map/all_to_all | solution.py:36
  85.7 5.8 %fusion.4 = f32[576,768]{1,0:T(8,128)} fusion(bf16[576,2048]{1,0:T(8,128)(2,1)} %bitcast.8, bf16[1,2048,768]{2,1,0:T(8,128)(2,1)} %all-gather.8.cloned.1.call-done), kind=kOutput, calls=%fused_computation.15 | convolution fusion | flops 1811939328 | bytes 7274496 | tf_op jit(solution)/shard_map/asd,adf->asf/dot_general | solution.py:46
  91.5 10.7 %all-gather.6.cloned.1.call-done = bf16[1,2048,768]{2,1,0:T(8,128)(2,1)} async-done(((bf16[1,512,768]{2,1,0:T(8,128)(2,1)}), bf16[1,2048,768]{2,1,0:T(8,128)(2,1)}) %all-gather.6.cloned.1.call-update) | async-done | bytes 3145744 | tf_op jit(solution)/shard_map/all_gather | solution.py:55
  102.1 5.8 %fusion.8 = f32[576,768]{1,0:T(8,128)} fusion(bf16[576,2048]{1,0:T(8,128)(2,1)} %bitcast.8, bf16[1,2048,768]{2,1,0:T(8,128)(2,1)} %all-gather.6.cloned.1.call-done), kind=kOutput, calls=%fused_computation.19 | convolution fusion | flops 1811939328 | bytes 7274496 | tf_op jit(solution)/shard_map/asd,adf->asf/dot_general | solution.py:52
  108.0 31.3 %all-to-all-done = bf16[8,72,2048]{2,1,0:T(8,128)(2,1)S(1)} async-done(((bf16[8,72,2048]{2,1,0:T(8,128)(2,1)}), bf16[8,72,2048]{2,1,0:T(8,128)(2,1)S(1)}, u32[]{:S(2)}, u32[]{:S(2)}) %all-to-all-start) | async-done | bytes 2359328 | tf_op jit(solution)/shard_map/all_to_all | solution.py:36
  139.3 6.2 %fusion.14 = bf16[2048,768]{0,1:T(8,128)(2,1)} fusion(bf16[576,2048]{1,0:T(8,128)(2,1)S(1)} %bitcast.74, f32[576,768]{1,0:T(8,128)} %fusion.8, f32[576,768]{1,0:T(8,128)} %fusion.4), kind=kOutput, calls=%fused_computation.25 | convolution fusion | flops 1816166400 | bytes 9043968 | tf_op jit(solution)/shard_map/asd,asf->daf/dot_general | solution.py:89
  145.5 2.2 all-gather.4.cloned.1.call-done
  147.7 5.4 %multiply_convert_fusion.1 = (bf16[576,768]{1,0:T(8,128)(2,1)S(1)}, bf16[576,768]{1,0:T(8,128)(2,1)S(1)}) fusion(f32[576,768]{1,0:T(8,128)} %fusion.4, f32[576,768]{1,0:T(8,128)} %fusion.8, bf16[576,2048]{1,0:T(8,128)(2,1)S(1)} %bitcast.75, bf16[1,768,2048]{2,1,0:T(8,128)(2,1)} %all-gather.4.cloned.1.call-done), kind=kOutput, calls=%fused_computation.28 | convolution fusion | flops 1817690112 | bytes 10813440 | tf_op jit(solution)/shard_map/asd,afd->asf/dot_general | solution.py:66
  153.2 5.2 %fusion.13 = bf16[2048,768]{0,1:T(8,128)(2,1)S(1)} fusion(bf16[576,768]{1,0:T(8,128)(2,1)S(1)} %get-tuple-element.12, bf16[576,2048]{1,0:T(8,128)(2,1)} %bitcast.8), kind=kOutput, calls=%fused_computation.24 | convolution fusion | flops 1813512192 | bytes 6389760 | tf_op jit(solution)/shard_map/asd,asf->daf/dot_general | solution.py:88
  158.4 4.7 %fusion.12 = bf16[2048,768]{0,1:T(8,128)(2,1)S(1)} fusion(bf16[576,768]{1,0:T(8,128)(2,1)S(1)} %get-tuple-element.13, bf16[576,2048]{1,0:T(8,128)(2,1)} %bitcast.8), kind=kOutput, calls=%fused_computation.23 | convolution fusion | flops 1813512192 | bytes 6389760 | tf_op jit(solution)/shard_map/asd,asf->daf/dot_general | solution.py:87
  163.1 4.5 %pad_maximum_fusion = bf16[2048,2304]{0,1:T(8,128)(2,1)} fusion(bf16[2048,768]{0,1:T(8,128)(2,1)S(1)} %copy-done.3, bf16[2048,768]{0,1:T(8,128)(2,1)S(1)} %fusion.13, bf16[2048,768]{0,1:T(8,128)(2,1)S(1)} %fusion.12), kind=kLoop, calls=%fused_computation.5 | loop fusion | flops 28311552 | bytes 18874368 | tf_op jit(solution)/shard_map/concatenate | solution.py:91
  167.6 1.1 copy-done.7
  168.8 4.1 %fusion.2 = f32[576,2048]{1,0:T(8,128)S(1)} fusion(bf16[576,768]{1,0:T(8,128)(2,1)S(1)} %copy-done.7, bf16[1,2048,768]{2,1,0:T(8,128)(2,1)} %all-gather.8.cloned.1.call-done), kind=kOutput, calls=%fused_computation.13 | convolution fusion | flops 1811939328 | bytes 8749056 | tf_op jit(solution)/shard_map/asf,adf->asd/dot_general | solution.py:72
  172.9 3.4 %add_convert_fusion = bf16[576,2048]{1,0:T(8,128)(2,1)} fusion(f32[576,2048]{1,0:T(8,128)S(1)} %fusion.2, bf16[576,768]{1,0:T(8,128)(2,1)S(1)} %copy-done.9, bf16[1,2048,768]{2,1,0:T(8,128)(2,1)S(1)} %copy-done.5), kind=kOutput, calls=%fused_computation.9 | convolution fusion | flops 1814298624 | bytes 11108352 | tf_op jit(solution)/shard_map/asf,adf->asd/dot_general | solution.py:73
  176.3 4.8 %all-to-all-start.2 = ((bf16[8,72,2048]{2,1,0:T(8,128)(2,1)}), bf16[8,72,2048]{2,1,0:T(8,128)(2,1)S(1)}, u32[]{:S(2)}, u32[]{:S(2)}) async-start(bf16[8,72,2048]{2,1,0:T(8,128)(2,1)} %bitcast.76), calls=%async_computation.2 | async-start | bytes 4718592 | tf_op jit(solution)/shard_map/all_to_all | solution.py:79
  181.1 54.6 %all-to-all-done.2 = bf16[8,72,2048]{2,1,0:T(8,128)(2,1)S(1)} async-done(((bf16[8,72,2048]{2,1,0:T(8,128)(2,1)}), bf16[8,72,2048]{2,1,0:T(8,128)(2,1)S(1)}, u32[]{:S(2)}, u32[]{:S(2)}) %all-to-all-start.2) | async-done | bytes 2359328 | tf_op jit(solution)/shard_map/all_to_all | solution.py:79
  235.8 3.3 %gather_fusion.3 = bf16[512,2048]{1,0:T(8,128)(2,1)} fusion(bf16[576,2048]{1,0:T(8,128)(2,1)S(1)} %bitcast.71, s32[1024]{0:T(1024)S(1)} %pad_clamp_fusion), kind=kCustom, calls=%fused_computation.3 | custom fusion | bytes 4196352 | tf_op jit(solution)/shard_map/gather | solution.py:80
  239.1 2.8 %gather.21 = bf16[128,4,2048]{2,1,0:T(4,128)(2,1)S(1)} reshape(bf16[512,2048]{1,0:T(8,128)(2,1)} %gather_fusion.3) | data formatting | bytes 4194304 | tf_op jit(solution)/shard_map/gather | solution.py:80
  241.9 4.0 %reduce_sum.25 = bf16[128,2048]{1,0:T(8,128)(2,1)} reduce(bf16[128,4,2048]{2,1,0:T(4,128)(2,1)S(1)} %gather.21, bf16[]{:T(256)} %constant.36.clone.1), dimensions={1}, to_apply=%region_4.5 | reduce | flops 786432 | bytes 2621442 | tf_op jit(solution)/shard_map/reduce_sum | solution.py:81
  245.9 16.8 %reduce-scatter.2.cloned.1.call-done = bf16[512,2304]{0,1:T(8,128)(2,1)} async-done(((bf16[2048,2304]{0,1:T(8,128)(2,1)}), bf16[512,2304]{0,1:T(8,128)(2,1)}) %reduce-scatter.2.cloned.1.call-update) | async-done | bytes 2359312 | tf_op jit(solution)/shard_map/reduce_scatter | solution.py:90
  262.7 2.7 slice_bitcast_fusion
  265.4 1.2 copy.18
  266.5 1.2 copy.17
  (49 shorter events, 5.1 us)
Async XLA Ops:
  7.2 7.5 %copy-start = (bf16[128,2048]{1,0:T(8,128)(2,1)S(1)}, bf16[128,2048]{1,0:T(8,128)(2,1)}, u32[]{:S(2)}) copy-start(bf16[128,2048]{1,0:T(8,128)(2,1)} %param.7) | copy-start | bytes 1572868
  7.2 78.5 %all-gather.8.cloned.1.call-start = ((), (), s32[]{:S(2)}) async-start(), calls=%async_computation.6 | async-start | bytes 3932160 | tf_op jit(solution)/shard_map/all_gather | solution.py:49
  7.9 94.2 %all-gather.6.cloned.1.call-start = ((), (), s32[]{:S(2)}) async-start(), calls=%async_computation.5 | async-start | bytes 3932160 | tf_op jit(solution)/shard_map/all_gather | solution.py:55
  19.7 6.5 %copy-start.4 = (f32[128,4]{0,1:T(4,128)S(1)}, f32[128,4]{0,1:T(4,128)}, u32[]{:S(2)}) copy-start(f32[128,4]{0,1:T(4,128)} %param.10) | copy-start | bytes 6148
  19.7 61.2 %all-to-all-start.1 = ((bf16[8,72,2048]{2,1,0:T(8,128)(2,1)}), bf16[8,72,2048]{2,1,0:T(8,128)(2,1)}, u32[]{:S(2)}, u32[]{:S(2)}) async-start(bf16[8,72,2048]{2,1,0:T(8,128)(2,1)} %broadcast_select_fusion), calls=%async_computation.1 | async-start | bytes 4718592 | tf_op jit(solution)/shard_map/all_to_all | solution.py:35
  26.2 4.3 %copy-start.2 = (bf16[128,2048]{1,0:T(8,128)(2,1)S(1)}, bf16[128,2048]{1,0:T(8,128)(2,1)}, u32[]{:S(2)}) copy-start(bf16[128,2048]{1,0:T(8,128)(2,1)} %param.8) | copy-start | bytes 1572868
  81.0 58.3 %all-to-all-start = ((bf16[8,72,2048]{2,1,0:T(8,128)(2,1)}), bf16[8,72,2048]{2,1,0:T(8,128)(2,1)S(1)}, u32[]{:S(2)}, u32[]{:S(2)}) async-start(bf16[8,72,2048]{2,1,0:T(8,128)(2,1)} %fusion.1), calls=%async_computation | async-start | bytes 4718592 | tf_op jit(solution)/shard_map/all_to_all | solution.py:36
  84.7 63.0 %all-gather.4.cloned.1.call-start = ((), (), s32[]{:S(2)}) async-start(), calls=%async_computation.4 | async-start | bytes 3932160 | tf_op jit(solution)/shard_map/all_gather | solution.py:61
  85.4 177.2 %reduce-scatter.2.cloned.1.call-start = ((), (), s32[]{:S(2)}) async-start(), calls=%async_computation.7 | async-start | bytes 11796480 | tf_op jit(solution)/shard_map/reduce_scatter | solution.py:90
  153.1 5.2 %copy-start.8 = (bf16[576,768]{1,0:T(8,128)(2,1)}, bf16[576,768]{1,0:T(8,128)(2,1)S(1)}, u32[]{:S(2)}) copy-start(bf16[576,768]{1,0:T(8,128)(2,1)S(1)} %get-tuple-element.12) | copy-start | bytes 2654212
  153.2 5.2 %copy-start.6 = (bf16[576,768]{1,0:T(8,128)(2,1)}, bf16[576,768]{1,0:T(8,128)(2,1)S(1)}, u32[]{:S(2)}) copy-start(bf16[576,768]{1,0:T(8,128)(2,1)S(1)} %get-tuple-element.13) | copy-start | bytes 2654212
  158.4 4.7 %copy-start.3 = (bf16[2048,768]{0,1:T(8,128)(2,1)S(1)}, bf16[2048,768]{0,1:T(8,128)(2,1)}, u32[]{:S(2)}) copy-start(bf16[2048,768]{0,1:T(8,128)(2,1)} %fusion.14) | copy-start | bytes 9437188
  167.6 1.2 copy-start.7
  168.8 4.1 %copy-start.5 = (bf16[1,2048,768]{2,1,0:T(8,128)(2,1)S(1)}, bf16[1,2048,768]{2,1,0:T(8,128)(2,1)}, u32[]{:S(2)}) copy-start(bf16[1,2048,768]{2,1,0:T(8,128)(2,1)} %all-gather.6.cloned.1.call-done) | copy-start | bytes 9437188
  168.8 4.1 %copy-start.9 = (bf16[576,768]{1,0:T(8,128)(2,1)S(1)}, bf16[576,768]{1,0:T(8,128)(2,1)}, u32[]{:S(2)}) copy-start(bf16[576,768]{1,0:T(8,128)(2,1)} %copy-done.8) | copy-start | bytes 2654212
  176.3 59.5 %all-to-all-start.2 = ((bf16[8,72,2048]{2,1,0:T(8,128)(2,1)}), bf16[8,72,2048]{2,1,0:T(8,128)(2,1)S(1)}, u32[]{:S(2)}, u32[]{:S(2)}) async-start(bf16[8,72,2048]{2,1,0:T(8,128)(2,1)} %bitcast.76), calls=%async_computation.2 | async-start | bytes 4718592 | tf_op jit(solution)/shard_map/all_to_all | solution.py:79
  262.7 5.0 %copy-start.1 = (bf16[128,2048]{1,0:T(8,128)(2,1)S(1)}, bf16[128,2048]{1,0:T(8,128)(2,1)}, u32[]{:S(2)}) copy-start(bf16[128,2048]{1,0:T(8,128)(2,1)} %param.7) | copy-start | bytes 1572868
Sparse Core Ops, SparseCore 0:
  9.8 46.5 all-gather.7
  58.3 43.8 all-gather.5
  104.0 43.6 all-gather.3
  167.7 94.8 reduce-scatter.1
where the time goes:
time: 275 us; the launch traced here: 274 us
  waiting for transfers between devices  163 us (59%)
  matrix products  40.7 us (15%)
  local copies, waits for them, and re-layouts  27.4 us (10%)
  starting transfers between devices  15.4 us (6%)
  other arithmetic  14.1 us (5%)
  between operations  14 us (5%)
    all_to_all x1, waiting for transfers between devices, local(): lax.all_to_all(send_back, 'expert', split_axis=0, concat_axis=0, tiled=True)  54.6 us
    all_to_all x1, waiting for transfers between devices, local(): lax.all_to_all(send_x, 'expert', split_axis=0, concat_axis=0, tiled=True)  45 us
    all_to_all x1, waiting for transfers between devices, local(): lax.all_to_all(send_dy, 'expert', split_axis=0, concat_axis=0, tiled=True)  31.3 us
    reduce_scatter x1, waiting for transfers between devices, local(): lax.psum_scatter(jnp.concatenate([term_gate.reshape(lax.axis_size('dp') *...  16.8 us
    all_gather x1, waiting for transfers between devices, local(): lax.all_gather(w_up, 'dp', axis=1, tiled=True)  10.7 us
    all_to_all x1, starting transfers between devices, local(): lax.all_to_all(send_x, 'expert', split_axis=0, concat_axis=0, tiled=True)  6.49 us
    dot_general x1, matrix products, local(): jnp.einsum('asd,asf->daf', slot_dy, activated, preferred_element_type=jnp...  6.23 us
    gather x2, local copies, waits for them, and re-layouts, local(): returned.reshape(expert_count * capacity, model_width)[slot_of]  6.13 us
  transfers between devices with their start and end apart: 7, of which 6 were waited for; matrix products, arithmetic and copies ran while one was open for 20% of the time, Pallas kernels for 0%

commit v1 on v0

--- a/solution.py
+++ b/solution.py
@@ -2,6 +2,34 @@
 import jax.numpy as jnp
 from jax import lax
 from jax.sharding import PartitionSpec as P
+
+
+def check_cubes(own_rows, axis_k, vec):
+    parts_out, near = (own_rows.shape[:axis_k], own_rows.shape[axis_k + 1 :])
+    t1 = own_rows.reshape(*parts_out, vec, -1, *near)
+    return jnp.moveaxis(t1, axis_k, 0)
+
+
+def start_chunk(tile_in, join_dim):
+    u_next = list(tile_in.shape[1:])
+    u_next[join_dim] *= tile_in.shape[0]
+    return jnp.moveaxis(tile_in, 0, join_dim).reshape(u_next)
+
+
+def divide_patches(here_x, ax_name, array_in, my_tile):
+    y1 = lax.axis_size(ax_name)
+    tile_out = lax.axis_index(ax_name)
+    z, frame_out = (y1, tile_out)
+    arr_next = check_cubes(here_x, array_in, z)
+    s_next = arr_next
+    j0 = 1
+    while j0 < z:
+        inter, e_now = ((frame_out + j0) % z, (frame_out - j0) % z)
+        k_now = lax.dynamic_index_in_dim(arr_next, inter, 0)
+        arr_out = lax.ppermute(k_now, ax_name, [(nth, (nth + j0) % z) for nth in range(z)])
+        s_next = lax.dynamic_update_slice_in_dim(s_next, arr_out, e_now, axis=0)
+        j0 += 1
+    return start_chunk(s_next, my_tile)
 
 
 def local(tokens, out_grad, routes, gate_values, w_gate, w_up, w_down):
@@ -33,7 +61,7 @@
     send_dy = send_dy.reshape(expert_count, capacity, model_width)
     recv_x, recv_dy = (
         lax.all_to_all(send_x, "expert", split_axis=0, concat_axis=0, tiled=True),
-        lax.all_to_all(send_dy, "expert", split_axis=0, concat_axis=0, tiled=True),
+        divide_patches(send_dy, "expert", 0, 0),
     )
 
     def to_local(stacked):

time: 275 us -> 278 us (1.011)
  waiting for transfers between devices: 163 us -> 145 us
  starting transfers between devices: 15.4 us -> 31.4 us
  local copies, waits for them, and re-layouts: 27.4 us -> 36.6 us
  matrix products: 40.7 us -> 37.6 us
    ppermute x0 -> x7, waiting for transfers between devices: none -> 56.1 us  [divide_patches(): lax.ppermute(k_now, ax_name, [(nth, (nth + j0) % z) for nth in range(z)])]
    all_to_all x1, waiting for transfers between devices: 45 us -> 0.01 us  [local(): lax.all_to_all(send_x, 'expert', split_axis=0, concat_axis=0, tiled=True)]
    all_to_all x1 -> x0, waiting for transfers between devices: 31.3 us -> none  [local(): lax.all_to_all(send_dy, 'expert', split_axis=0, concat_axis=0, tiled=True)]
    ppermute x0 -> x7, starting transfers between devices: none -> 17.9 us  [divide_patches(): lax.ppermute(k_now, ax_name, [(nth, (nth + j0) % z) for nth in range(z)])]
    all_gather x1, waiting for transfers between devices: 2.22 us -> 14.2 us  [local(): lax.all_gather(w_down, 'dp', axis=2, tiled=True)]
    all_gather x1, waiting for transfers between devices: 10.7 us -> 0.01 us  [local(): lax.all_gather(w_up, 'dp', axis=1, tiled=True)]
    dynamic_update_slice x0 -> x6, local copies, waits for them, and re-layouts: none -> 4.4 us  [divide_patches(): s_next = lax.dynamic_update_slice_in_dim(s_next, arr_out, e_now, axis=0)]
    all_to_all x1 -> x0, starting transfers between devices: 3.7 us -> none  [local(): lax.all_to_all(send_dy, 'expert', split_axis=0, concat_axis=0, tiled=True)]
  transfers between devices with their start and end apart: 7 -> 13, of which waited for: 6 -> 7; matrix products, arithmetic and copies ran while one was open for 20% -> 21% of each run, Pallas kernels for 0% -> 0%
where the time goes in v1:
time: 278 us; the launch traced here: 277 us
  waiting for transfers between devices  145 us (52%)
  matrix products  37.6 us (14%)
  local copies, waits for them, and re-layouts  36.6 us (13%)
  starting transfers between devices  31.4 us (11%)
  between operations  14.1 us (5%)
  other arithmetic  12.6 us (5%)
    ppermute x7, waiting for transfers between devices, divide_patches(): lax.ppermute(k_now, ax_name, [(nth, (nth + j0) % z) for nth in range(z)])  56.1 us
    all_to_all x1, waiting for transfers between devices, local(): lax.all_to_all(send_back, 'expert', split_axis=0, concat_axis=0, tiled=True)  54.6 us
    reduce_scatter x1, waiting for transfers between devices, local(): lax.psum_scatter(jnp.concatenate([term_gate.reshape(lax.axis_size('dp') *...  18.2 us
    ppermute x7, starting transfers between devices, divide_patches(): lax.ppermute(k_now, ax_name, [(nth, (nth + j0) % z) for nth in range(z)])  17.9 us
    all_gather x1, waiting for transfers between devices, local(): lax.all_gather(w_down, 'dp', axis=2, tiled=True)  14.2 us
    unnamed x32, local copies, waits for them, and re-layouts  6.99 us
    all_to_all x1, starting transfers between devices, local(): lax.all_to_all(send_back, 'expert', split_axis=0, concat_axis=0, tiled=True)  6.86 us
    all_to_all x1, starting transfers between devices, local(): lax.all_to_all(send_x, 'expert', split_axis=0, concat_axis=0, tiled=True)  6.49 us
  transfers between devices with their start and end apart: 13, of which 7 were waited for; matrix products, arithmetic and copies ran while one was open for 21% of the time, Pallas kernels for 0%

profile of v1, /device:TPU:0, one launch (start us, length us, event | category | flops | bytes accessed | tf_op | source)
XLA Modules:
  0.0 277.5 jit_solution(16528348888256378391)
XLA Ops:
  12.1 2.4 scatter_custom_fusion
  14.7 3.4 %gather_fusion.2 = bf16[576,2048]{1,0:T(8,128)(2,1)S(1)} fusion(bf16[128,2048]{1,0:T(8,128)(2,1)S(1)} %copy-done, s32[1024]{0:T(1024)S(1)} %get-tuple-element.26), kind=kCustom, calls=%fused_computation.2 | custom fusion | bytes 4720896 | tf_op jit(solution)/shard_map/gather | solution.py:57
  18.1 1.7 broadcast_select_fusion
  19.8 6.5 %all-to-all-start = ((bf16[8,72,2048]{2,1,0:T(8,128)(2,1)}), bf16[8,72,2048]{2,1,0:T(8,128)(2,1)}, u32[]{:S(2)}, u32[]{:S(2)}) async-start(bf16[8,72,2048]{2,1,0:T(8,128)(2,1)} %broadcast_select_fusion), calls=%async_computation | async-start | bytes 4718592 | tf_op jit(solution)/shard_map/all_to_all | solution.py:63
  27.1 3.4 %gather_fusion.1 = bf16[576,2048]{1,0:T(8,128)(2,1)S(1)} fusion(bf16[128,2048]{1,0:T(8,128)(2,1)S(1)} %copy-done.2, s32[1024]{0:T(1024)S(1)} %get-tuple-element.26), kind=kCustom, calls=%fused_computation.1 | custom fusion | bytes 4720896 | tf_op jit(solution)/shard_map/gather | solution.py:58
  30.8 4.0 %gather_fusion = f32[576]{0:T(1024)S(1)} fusion(f32[512]{0:T(512)S(1)} %reshape.189, s32[1024]{0:T(1024)S(1)} %get-tuple-element.27), kind=kCustom, calls=%fused_computation | custom fusion | bytes 6912 | tf_op jit(solution)/shard_map/gather | solution.py:58
  35.4 1.4 copy-done.3
  37.4 35.1 %collective-permute-done = bf16[1,1,72,2048]{3,2,0,1:T(8,128)(2,1)S(1)} collective-permute-done((bf16[1,1,72,2048]{3,2,0,1:T(8,128)(2,1)S(1)}, bf16[1,1,72,2048]{3,2,0,1:T(8,128)(2,1)S(1)}, u32[]{:S(2)}, u32[]{:S(2)}) %collective-permute-start) | collective-permute-done | bytes 294944 | tf_op jit(solution)/shard_map/ppermute | solution.py:29
  72.5 2.4 constant_dynamic-slice_fusion
  74.9 9.8 %collective-permute-start.2 = (bf16[1,1,72,2048]{3,2,0,1:T(8,128)(2,1)S(1)}, bf16[1,1,72,2048]{3,2,0,1:T(8,128)(2,1)S(1)}, u32[]{:S(2)}, u32[]{:S(2)}) collective-permute-start(bf16[1,1,72,2048]{3,2,0,1:T(8,128)(2,1)S(1)} %get-tuple-element.21), channel_id=1, source_target_pairs={{0,3},{1,4},{2,5},{3,6},{4,7},{5,0},{6,1},{7,2},{8,11},{9,12},{10,... | collective-permute-start | bytes 884744 | tf_op jit(solution)/shard_map/ppermute | solution.py:29
  84.7 2.5 collective-permute-start.3
  87.2 2.2 collective-permute-start.4
  89.3 2.9 %collective-permute-start.5 = (bf16[1,1,72,2048]{3,2,0,1:T(8,128)(2,1)S(1)}, bf16[1,1,72,2048]{3,2,0,1:T(8,128)(2,1)S(1)}, u32[]{:S(2)}, u32[]{:S(2)}) collective-permute-start(bf16[1,1,72,2048]{3,2,0,1:T(8,128)(2,1)S(1)} %get-tuple-element.18), channel_id=1, source_target_pairs={{0,6},{1,7},{2,0},{3,1},{4,2},{5,3},{6,4},{7,5},{8,14},{9,15},{10,... | collective-permute-start | bytes 884744 | tf_op jit(solution)/shard_map/ppermute | solution.py:29
  93.0 19.0 %collective-permute-done.2 = bf16[1,1,72,2048]{3,2,0,1:T(8,128)(2,1)S(1)} collective-permute-done((bf16[1,1,72,2048]{3,2,0,1:T(8,128)(2,1)S(1)}, bf16[1,1,72,2048]{3,2,0,1:T(8,128)(2,1)S(1)}, u32[]{:S(2)}, u32[]{:S(2)}) %collective-permute-start.2) | collective-permute-done | bytes 294944 | tf_op jit(solution)/shard_map/ppermute | solution.py:29
  115.3 1.5 collective-permute-done.6
  117.6 5.8 %fusion.4 = f32[576,768]{1,0:T(8,128)} fusion(bf16[576,2048]{1,0:T(8,128)(2,1)} %bitcast.8, bf16[1,2048,768]{2,1,0:T(8,128)(2,1)} %all-gather.8.cloned.1.call-done), kind=kOutput, calls=%fused_computation.15 | convolution fusion | flops 1811939328 | bytes 7274496 | tf_op jit(solution)/shard_map/asd,adf->asf/dot_general | solution.py:74
  123.5 4.7 %fusion.8 = f32[576,768]{1,0:T(8,128)S(1)} fusion(bf16[576,2048]{1,0:T(8,128)(2,1)} %bitcast.8, bf16[1,2048,768]{2,1,0:T(8,128)(2,1)} %all-gather.6.cloned.1.call-done), kind=kOutput, calls=%fused_computation.19 | convolution fusion | flops 1811939328 | bytes 7274496 | tf_op jit(solution)/shard_map/asd,adf->asf/dot_general | solution.py:80
  129.4 4.1 %fusion.14 = bf16[2048,768]{0,1:T(8,128)(2,1)} fusion(bf16[576,2048]{1,0:T(8,128)(2,1)S(1)} %bitcast.73, f32[576,768]{1,0:T(8,128)S(1)} %fusion.8, f32[576,768]{1,0:T(8,128)S(1)} %copy-done.10), kind=kOutput, calls=%fused_computation.25 | convolution fusion | flops 1816166400 | bytes 9043968 | tf_op jit(solution)/shard_map/asd,asf->daf/dot_general | solution.py:117
  133.5 14.2 %all-gather.4.cloned.1.call-done = bf16[1,768,2048]{2,1,0:T(8,128)(2,1)} async-done(((bf16[1,768,512]{2,1,0:T(8,128)(2,1)}), bf16[1,768,2048]{2,1,0:T(8,128)(2,1)}) %all-gather.4.cloned.1.call-update) | async-done | bytes 3145744 | tf_op jit(solution)/shard_map/all_gather | solution.py:89
  147.8 5.4 %multiply_convert_fusion.1 = (bf16[576,768]{1,0:T(8,128)(2,1)S(1)}, bf16[576,768]{1,0:T(8,128)(2,1)S(1)}) fusion(f32[576,768]{1,0:T(8,128)} %fusion.4, f32[576,768]{1,0:T(8,128)} %copy-done.11, bf16[576,2048]{1,0:T(8,128)(2,1)S(1)} %bitcast.74, bf16[1,768,2048]{2,1,0:T(8,128)(2,1)} %all-gather.4.cloned.1.call-done), kind=kOutput, calls=%fused_computation.28 | convolution fusion | flops 1817690112 | bytes 10813440 | tf_op jit(solution)/shard_map/asd,afd->asf/dot_general | solution.py:94
  153.2 5.2 %fusion.13 = bf16[2048,768]{0,1:T(8,128)(2,1)S(1)} fusion(bf16[576,768]{1,0:T(8,128)(2,1)S(1)} %get-tuple-element.12, bf16[576,2048]{1,0:T(8,128)(2,1)} %bitcast.8), kind=kOutput, calls=%fused_computation.24 | convolution fusion | flops 1813512192 | bytes 6389760 | tf_op jit(solution)/shard_map/asd,asf->daf/dot_general | solution.py:116
  158.4 4.7 %fusion.12 = bf16[2048,768]{0,1:T(8,128)(2,1)S(1)} fusion(bf16[576,768]{1,0:T(8,128)(2,1)S(1)} %get-tuple-element.13, bf16[576,2048]{1,0:T(8,128)(2,1)} %bitcast.8), kind=kOutput, calls=%fused_computation.23 | convolution fusion | flops 1813512192 | bytes 6389760 | tf_op jit(solution)/shard_map/asd,asf->daf/dot_general | solution.py:115
  163.1 4.4 %pad_maximum_fusion = bf16[2048,2304]{0,1:T(8,128)(2,1)} fusion(bf16[2048,768]{0,1:T(8,128)(2,1)S(1)} %copy-done.5, bf16[2048,768]{0,1:T(8,128)(2,1)S(1)} %fusion.13, bf16[2048,768]{0,1:T(8,128)(2,1)S(1)} %fusion.12), kind=kLoop, calls=%fused_computation.5 | loop fusion | flops 28311552 | bytes 18874368 | tf_op jit(solution)/shard_map/concatenate | solution.py:119
  168.7 4.1 %fusion.2 = f32[576,2048]{1,0:T(8,128)S(1)} fusion(bf16[576,768]{1,0:T(8,128)(2,1)S(1)} %copy-done.9, bf16[1,2048,768]{2,1,0:T(8,128)(2,1)} %all-gather.8.cloned.1.call-done), kind=kOutput, calls=%fused_computation.13 | convolution fusion | flops 1811939328 | bytes 8749056 | tf_op jit(solution)/shard_map/asf,adf->asd/dot_general | solution.py:100
  172.8 3.5 %add_convert_fusion = bf16[576,2048]{1,0:T(8,128)(2,1)} fusion(f32[576,2048]{1,0:T(8,128)S(1)} %fusion.2, bf16[576,768]{1,0:T(8,128)(2,1)S(1)} %copy-done.13, bf16[1,2048,768]{2,1,0:T(8,128)(2,1)S(1)} %copy-done.7), kind=kOutput, calls=%fused_computation.9 | convolution fusion | flops 1814298624 | bytes 11108352 | tf_op jit(solution)/shard_map/asf,adf->asd/dot_general | solution.py:101
  176.4 6.9 %all-to-all-start.1 = ((bf16[8,72,2048]{2,1,0:T(8,128)(2,1)}), bf16[8,72,2048]{2,1,0:T(8,128)(2,1)S(1)}, u32[]{:S(2)}, u32[]{:S(2)}) async-start(bf16[8,72,2048]{2,1,0:T(8,128)(2,1)} %bitcast.75), calls=%async_computation.1 | async-start | bytes 4718592 | tf_op jit(solution)/shard_map/all_to_all | solution.py:107
  183.2 54.6 %all-to-all-done.1 = bf16[8,72,2048]{2,1,0:T(8,128)(2,1)S(1)} async-done(((bf16[8,72,2048]{2,1,0:T(8,128)(2,1)}), bf16[8,72,2048]{2,1,0:T(8,128)(2,1)S(1)}, u32[]{:S(2)}, u32[]{:S(2)}) %all-to-all-start.1) | async-done | bytes 2359328 | tf_op jit(solution)/shard_map/all_to_all | solution.py:107
  237.9 3.3 %gather_fusion.3 = bf16[512,2048]{1,0:T(8,128)(2,1)} fusion(bf16[576,2048]{1,0:T(8,128)(2,1)S(1)} %bitcast.70, s32[1024]{0:T(1024)S(1)} %pad_clamp_fusion), kind=kCustom, calls=%fused_computation.3 | custom fusion | bytes 4196352 | tf_op jit(solution)/shard_map/gather | solution.py:108
  241.1 2.7 gather.21
  243.9 3.9 %reduce_sum.25 = bf16[128,2048]{1,0:T(8,128)(2,1)} reduce(bf16[128,4,2048]{2,1,0:T(4,128)(2,1)S(1)} %gather.21, bf16[]{:T(256)} %constant.142.clone.1), dimensions={1}, to_apply=%region_4.5 | reduce | flops 786432 | bytes 2621442 | tf_op jit(solution)/shard_map/reduce_sum | solution.py:109
  247.7 18.2 %reduce-scatter.2.cloned.1.call-done = bf16[512,2304]{0,1:T(8,128)(2,1)} async-done(((bf16[2048,2304]{0,1:T(8,128)(2,1)}), bf16[512,2304]{0,1:T(8,128)(2,1)}) %reduce-scatter.2.cloned.1.call-update) | async-done | bytes 2359312 | tf_op jit(solution)/shard_map/reduce_scatter | solution.py:118
  265.9 2.7 slice_bitcast_fusion
  (77 shorter events, 16.8 us)
Async XLA Ops:
  7.2 7.5 %copy-start = (bf16[128,2048]{1,0:T(8,128)(2,1)S(1)}, bf16[128,2048]{1,0:T(8,128)(2,1)}, u32[]{:S(2)}) copy-start(bf16[128,2048]{1,0:T(8,128)(2,1)} %param.7) | copy-start | bytes 1572868
  7.2 110.4 %all-gather.8.cloned.1.call-start = ((), (), s32[]{:S(2)}) async-start(), calls=%async_computation.5 | async-start | bytes 3932160 | tf_op jit(solution)/shard_map/all_gather | solution.py:77
  7.9 115.5 %all-gather.6.cloned.1.call-start = ((), (), s32[]{:S(2)}) async-start(), calls=%async_computation.4 | async-start | bytes 3932160 | tf_op jit(solution)/shard_map/all_gather | solution.py:83
  19.8 7.3 %copy-start.2 = (bf16[128,2048]{1,0:T(8,128)(2,1)S(1)}, bf16[128,2048]{1,0:T(8,128)(2,1)}, u32[]{:S(2)}) copy-start(bf16[128,2048]{1,0:T(8,128)(2,1)} %param.8) | copy-start | bytes 1572868
  19.8 97.8 %all-to-all-start = ((bf16[8,72,2048]{2,1,0:T(8,128)(2,1)}), bf16[8,72,2048]{2,1,0:T(8,128)(2,1)}, u32[]{:S(2)}, u32[]{:S(2)}) async-start(bf16[8,72,2048]{2,1,0:T(8,128)(2,1)} %broadcast_select_fusion), calls=%async_computation | async-start | bytes 4718592 | tf_op jit(solution)/shard_map/all_to_all | solution.py:63
  26.3 121.5 %all-gather.4.cloned.1.call-start = ((), (), s32[]{:S(2)}) async-start(), calls=%async_computation.3 | async-start | bytes 3932160 | tf_op jit(solution)/shard_map/all_gather | solution.py:89
  27.0 238.9 %reduce-scatter.2.cloned.1.call-start = ((), (), s32[]{:S(2)}) async-start(), calls=%async_computation.6 | async-start | bytes 11796480 | tf_op jit(solution)/shard_map/reduce_scatter | solution.py:118
  27.1 3.4 %copy-start.6 = (f32[128,4]{0,1:T(4,128)S(1)}, f32[128,4]{0,1:T(4,128)}, u32[]{:S(2)}) copy-start(f32[128,4]{0,1:T(4,128)} %param.10) | copy-start | bytes 6148
  35.4 1.4 copy-start.3
  36.9 35.7 %collective-permute-start = (bf16[1,1,72,2048]{3,2,0,1:T(8,128)(2,1)S(1)}, bf16[1,1,72,2048]{3,2,0,1:T(8,128)(2,1)S(1)}, u32[]{:S(2)}, u32[]{:S(2)}) collective-permute-start(bf16[1,1,72,2048]{3,2,0,1:T(8,128)(2,1)S(1)} %constant_dynamic-slice_fusion.6), channel_id=1, source_target_pairs={{0,1},{1,2},{2,3},{3,4},{4,5},{5,6},{6,7},{7,0},{8,9},{9,10},{10,1... | collective-permute-start | bytes 884744 | tf_op jit(solution)/shard_map/ppermute | solution.py:29
  74.9 17.4 %collective-permute-start.1 = (bf16[1,1,72,2048]{3,2,0,1:T(8,128)(2,1)S(1)}, bf16[1,1,72,2048]{3,2,0,1:T(8,128)(2,1)S(1)}, u32[]{:S(2)}, u32[]{:S(2)}) collective-permute-start(bf16[1,1,72,2048]{3,2,0,1:T(8,128)(2,1)S(1)} %get-tuple-element.22), channel_id=1, source_target_pairs={{0,2},{1,3},{2,4},{3,5},{4,6},{5,7},{6,0},{7,1},{8,10},{9,11},{10,... | collective-permute-start | bytes 884744 | tf_op jit(solution)/shard_map/ppermute | solution.py:29
  74.9 37.1 %collective-permute-start.2 = (bf16[1,1,72,2048]{3,2,0,1:T(8,128)(2,1)S(1)}, bf16[1,1,72,2048]{3,2,0,1:T(8,128)(2,1)S(1)}, u32[]{:S(2)}, u32[]{:S(2)}) collective-permute-start(bf16[1,1,72,2048]{3,2,0,1:T(8,128)(2,1)S(1)} %get-tuple-element.21), channel_id=1, source_target_pairs={{0,3},{1,4},{2,5},{3,6},{4,7},{5,0},{6,1},{7,2},{8,11},{9,12},{10,... | collective-permute-start | bytes 884744 | tf_op jit(solution)/shard_map/ppermute | solution.py:29
  84.7 28.4 %collective-permute-start.3 = (bf16[1,1,72,2048]{3,2,0,1:T(8,128)(2,1)S(1)}, bf16[1,1,72,2048]{3,2,0,1:T(8,128)(2,1)S(1)}, u32[]{:S(2)}, u32[]{:S(2)}) collective-permute-start(bf16[1,1,72,2048]{3,2,0,1:T(8,128)(2,1)S(1)} %get-tuple-element.20), channel_id=1, source_target_pairs={{0,4},{1,5},{2,6},{3,7},{4,0},{5,1},{6,2},{7,3},{8,12},{9,13},{10,... | collective-permute-start | bytes 884744 | tf_op jit(solution)/shard_map/ppermute | solution.py:29
  87.2 26.7 %collective-permute-start.4 = (bf16[1,1,72,2048]{3,2,0,1:T(8,128)(2,1)S(1)}, bf16[1,1,72,2048]{3,2,0,1:T(8,128)(2,1)S(1)}, u32[]{:S(2)}, u32[]{:S(2)}) collective-permute-start(bf16[1,1,72,2048]{3,2,0,1:T(8,128)(2,1)S(1)} %get-tuple-element.19), channel_id=1, source_target_pairs={{0,5},{1,6},{2,7},{3,0},{4,1},{5,2},{6,3},{7,4},{8,13},{9,14},{10,... | collective-permute-start | bytes 884744 | tf_op jit(solution)/shard_map/ppermute | solution.py:29
  89.3 25.3 %collective-permute-start.5 = (bf16[1,1,72,2048]{3,2,0,1:T(8,128)(2,1)S(1)}, bf16[1,1,72,2048]{3,2,0,1:T(8,128)(2,1)S(1)}, u32[]{:S(2)}, u32[]{:S(2)}) collective-permute-start(bf16[1,1,72,2048]{3,2,0,1:T(8,128)(2,1)S(1)} %get-tuple-element.18), channel_id=1, source_target_pairs={{0,6},{1,7},{2,0},{3,1},{4,2},{5,3},{6,4},{7,5},{8,14},{9,15},{10,... | collective-permute-start | bytes 884744 | tf_op jit(solution)/shard_map/ppermute | solution.py:29
  92.3 24.6 %collective-permute-start.6 = (bf16[1,1,72,2048]{3,2,0,1:T(8,128)(2,1)S(1)}, bf16[1,1,72,2048]{3,2,0,1:T(8,128)(2,1)S(1)}, u32[]{:S(2)}, u32[]{:S(2)}) collective-permute-start(bf16[1,1,72,2048]{3,2,0,1:T(8,128)(2,1)S(1)} %get-tuple-element.17), channel_id=1, source_target_pairs={{0,7},{1,0},{2,1},{3,2},{4,3},{5,4},{6,5},{7,6},{8,15},{9,8},{10,9... | collective-permute-start | bytes 884744 | tf_op jit(solution)/shard_map/ppermute | solution.py:29
  123.4 6.0 %copy-start.4 = (bf16[8,1,72,2048]{3,2,0,1:T(8,128)(2,1)S(1)}, bf16[8,1,72,2048]{3,2,0,1:T(8,128)(2,1)}, u32[]{:S(2)}) copy-start(bf16[8,1,72,2048]{3,2,0,1:T(8,128)(2,1)} %constant_dynamic-update-slice_fusion) | copy-start | bytes 7077892
  123.5 6.0 %copy-start.10 = (f32[576,768]{1,0:T(8,128)S(1)}, f32[576,768]{1,0:T(8,128)}, u32[]{:S(2)}) copy-start(f32[576,768]{1,0:T(8,128)} %fusion.4) | copy-start | bytes 5308420
  128.2 1.2 copy-start.11
  153.2 5.2 %copy-start.12 = (bf16[576,768]{1,0:T(8,128)(2,1)}, bf16[576,768]{1,0:T(8,128)(2,1)S(1)}, u32[]{:S(2)}) copy-start(bf16[576,768]{1,0:T(8,128)(2,1)S(1)} %get-tuple-element.12) | copy-start | bytes 2654212
  153.2 5.2 %copy-start.8 = (bf16[576,768]{1,0:T(8,128)(2,1)}, bf16[576,768]{1,0:T(8,128)(2,1)S(1)}, u32[]{:S(2)}) copy-start(bf16[576,768]{1,0:T(8,128)(2,1)S(1)} %get-tuple-element.13) | copy-start | bytes 2654212
  158.4 4.7 %copy-start.5 = (bf16[2048,768]{0,1:T(8,128)(2,1)S(1)}, bf16[2048,768]{0,1:T(8,128)(2,1)}, u32[]{:S(2)}) copy-start(bf16[2048,768]{0,1:T(8,128)(2,1)} %fusion.14) | copy-start | bytes 9437188
  167.6 1.2 copy-start.9
  168.7 4.1 %copy-start.7 = (bf16[1,2048,768]{2,1,0:T(8,128)(2,1)S(1)}, bf16[1,2048,768]{2,1,0:T(8,128)(2,1)}, u32[]{:S(2)}) copy-start(bf16[1,2048,768]{2,1,0:T(8,128)(2,1)} %all-gather.6.cloned.1.call-done) | copy-start | bytes 9437188
  168.7 4.1 %copy-start.13 = (bf16[576,768]{1,0:T(8,128)(2,1)S(1)}, bf16[576,768]{1,0:T(8,128)(2,1)}, u32[]{:S(2)}) copy-start(bf16[576,768]{1,0:T(8,128)(2,1)} %copy-done.12) | copy-start | bytes 2654212
  176.4 61.5 %all-to-all-start.1 = ((bf16[8,72,2048]{2,1,0:T(8,128)(2,1)}), bf16[8,72,2048]{2,1,0:T(8,128)(2,1)S(1)}, u32[]{:S(2)}, u32[]{:S(2)}) async-start(bf16[8,72,2048]{2,1,0:T(8,128)(2,1)} %bitcast.75), calls=%async_computation.1 | async-start | bytes 4718592 | tf_op jit(solution)/shard_map/all_to_all | solution.py:107
  265.9 5.0 %copy-start.1 = (bf16[128,2048]{1,0:T(8,128)(2,1)S(1)}, bf16[128,2048]{1,0:T(8,128)(2,1)}, u32[]{:S(2)}) copy-start(bf16[128,2048]{1,0:T(8,128)(2,1)} %param.7) | copy-start | bytes 1572868
Sparse Core Ops, SparseCore 0:
  9.8 46.6 all-gather.7
  58.3 43.8 all-gather.5
  104.0 43.6 all-gather.3
  167.7 98.1 reduce-scatter.1
